TPU v7x, 32 devices: a whole 2x2x4 slice. The times are simulated.
32 devices in a mesh: walk: 2 (over y), row: 4 (over x, core), col: 4 (over z).
Axes of the slice: x: 2, y: 2, z: 4, core: 2. Of those that a mesh axis runs over, the one named last changes fastest.
Arguments:
- states: bfloat16 [2048, 512], P(('walk', 'row'), 'col'), parts along dimension 0, may hold values from -6 to 6
- spin: int32 [2048], P('walk'), parts along dimension 0, may hold values 0 or 1
- shift: int32 [32, 16], P('walk'), parts along dimension 0, may hold values from 0 to 26
- w_left: bfloat16 [2, 512, 512], replicated, may hold values from -0.25 to 0.25
- w_right: bfloat16 [2, 512, 512], replicated, may hold values from -0.25 to 0.25
- w_out: bfloat16 [2, 512, 512], replicated, may hold values from -0.25 to 0.25
- out_bias: float32 [2, 512], replicated, may hold values from -3 to 3
- shift_table: float32 [27, 512], replicated, may hold values from -6 to 6
- same_bias: float32 [512], replicated, may hold values from -6 to 6
- w_orbital: bfloat16 [512, 1024], P(None, 'col'), may hold values from -0.25 to 0.25
- envelope: float32 [2048, 1024], P(('walk', 'row'), 'col'), parts along dimension 0, may hold values from 0.05 to 0.5
- approx_inverse: float32 [2048, 1024], P(('walk', 'row'), 'col'), parts along dimension 0, may hold values from -0.1875 to 0.1875
Outputs:
- new_states: bfloat16 [2048, 512], P(('walk', 'row'), 'col'), parts along dimension 0
- refined: float32 [2048, 1024], P(('walk', 'row'), 'col'), parts along dimension 0
There are 2 independent parts, one for each index of `walk`. A program takes and returns all parts, laid end to end along the dimension named above; an argument that names none is the same for every part. Nothing has to cross between parts.
Inputs may be any that keep to these rules, and one draw needn't show every extreme that they name: `shift`: indices into shift_table.
All inputs are finite; a program needn't handle non-finite values.
Results may differ from a plain program's by a relative error of at most 0.0047.
Values may be sent and summed in bfloat16 or wider, within the bound.
No kernel may reach another device: no remote copies, remote signals or barrier semaphores. Data moves between devices by JAX's collectives and lax.ppermute only.
A program may use at most 64 MiB of HBM per device.

v0:
```python
import jax
import jax.numpy as jnp
from jax import lax
from jax.sharding import PartitionSpec as P

N = 1024
NB = 16
S = 27


def pair_messages(
    left_part, right_part, embedded_cols, same_spin, same_bias, weight_out, bias_out, block_size
):
    row_count = left_part.shape[0]
    step_rows = max(min(8, block_size), row_count // 8)
    turns = row_count // step_rows

    def one_step(running, turn_idx):
        begin_row = turn_idx * step_rows
        left_rows = lax.dynamic_slice_in_dim(left_part, begin_row, step_rows, 0)
        same_rows = lax.dynamic_slice_in_dim(same_spin, begin_row, step_rows, 0)
        shift_rows = lax.dynamic_index_in_dim(
            embedded_cols, begin_row // block_size, 0, keepdims=False
        )
        pre_act = (
            left_rows[:, None, :]
            + right_part[None, :, :]
            + shift_rows[None, :, :]
            + same_rows[:, :, None] * same_bias
        )
        gated_vals = jax.nn.silu(pre_act).astype(jnp.bfloat16)
        flat_rows = gated_vals.reshape(-1, gated_vals.shape[2])
        message = jnp.tanh(
            jnp.dot(flat_rows, weight_out, preferred_element_type=jnp.float32) + bias_out
        )
        message = message.reshape(step_rows, -1, message.shape[1])
        return (running, jnp.sum(message, axis=1))

    final_carry, stacked = lax.scan(one_step, jnp.int32(0), jnp.arange(turns, dtype=jnp.int32))
    return stacked.reshape(row_count, -1)


def per_device(
    states,
    spin,
    shift,
    w_left,
    w_right,
    w_out,
    out_bias,
    shift_table,
    same_bias,
    w_orbital,
    envelope,
    approx_inverse,
):
    col_devices = lax.axis_size("col")
    row_index = lax.axis_index("row")
    col_index = lax.axis_index("col")
    row_count = states.shape[0]
    col_count = N // col_devices
    block_size = N // NB
    row_begin = row_index * row_count
    col_begin = col_index * col_count
    row_spin = lax.dynamic_slice_in_dim(spin, row_begin, row_count, 0)
    col_spin = lax.dynamic_slice_in_dim(spin, col_begin, col_count, 0)
    same_spin = (row_spin[:, None] == col_spin[None, :]).astype(jnp.float32)
    local_shift = lax.dynamic_slice(
        shift,
        (row_begin // block_size, col_begin // block_size),
        (row_count // block_size, col_count // block_size),
    )
    onehot = (local_shift[:, :, None] == jnp.arange(S, dtype=jnp.int32)[None, None, :]).astype(
        jnp.float32
    )
    embedded = jnp.einsum("abs,sh->abh", onehot, shift_table, precision=lax.Precision.HIGHEST)
    embedded_cols = jnp.repeat(embedded, block_size, axis=1)
    full_rows = lax.all_gather(states, "col", axis=1, tiled=True)
    own_shard = states
    for layer_idx in range(w_left.shape[0]):
        left_part = jnp.dot(full_rows, w_left[layer_idx], preferred_element_type=jnp.float32)
        gathered = lax.all_gather(full_rows, "row", axis=0, tiled=True)
        col_states = lax.dynamic_slice_in_dim(gathered, col_begin, col_count, 0)
        right_part = jnp.dot(col_states, w_right[layer_idx], preferred_element_type=jnp.float32)
        pair_sums = pair_messages(
            left_part,
            right_part,
            embedded_cols,
            same_spin,
            same_bias,
            w_out[layer_idx],
            out_bias[layer_idx],
            block_size,
        )
        shares = lax.psum_scatter(pair_sums, "col", scatter_dimension=1, tiled=True) / N
        own_shard = (own_shard.astype(jnp.float32) + shares).astype(jnp.bfloat16)
        full_rows = lax.all_gather(own_shard, "col", axis=1, tiled=True)
    orbital = jnp.dot(full_rows, w_orbital, preferred_element_type=jnp.float32) * envelope
    panel = lax.all_gather(orbital, "col", axis=1, tiled=True)
    left_cols = panel
    product = jnp.dot(
        left_cols,
        lax.all_gather(approx_inverse, "row", axis=0, tiled=True),
        precision=lax.Precision.HIGHEST,
        preferred_element_type=jnp.float32,
    )
    row_ids = row_begin + jnp.arange(row_count, dtype=jnp.int32)
    col_ids = col_begin + jnp.arange(col_count, dtype=jnp.int32)
    identity_part = (row_ids[:, None] == col_ids[None, :]).astype(jnp.float32)
    residual_part = 2.0 * identity_part - product
    inverse_panel = lax.all_gather(approx_inverse, "col", axis=1, tiled=True)
    left_cols = inverse_panel
    refined = jnp.dot(
        left_cols,
        lax.all_gather(residual_part, "row", axis=0, tiled=True),
        precision=lax.Precision.HIGHEST,
        preferred_element_type=jnp.float32,
    )
    return (own_shard, refined)


def solution(mesh):
    placed = (
        P(("walk", "row"), "col"),
        P("walk"),
        P("walk", None),
        P(),
        P(),
        P(),
        P(),
        P(),
        P(),
        P(None, "col"),
        P(("walk", "row"), "col"),
        P(("walk", "row"), "col"),
    )
    return jax.shard_map(
        per_device,
        mesh=mesh,
        in_specs=placed,
        out_specs=(P(("walk", "row"), "col"), P(("walk", "row"), "col")),
        check_vma=False,
    )
```

profile of v0, /device:TPU:0, one launch (start us, length us, event | category | flops | bytes accessed | tf_op | source)
XLA Modules:
  0.0 488.7 jit_solution(9008401775313217856)
XLA Ops:
  7.2 16.7 %all_gather.27 = bf16[256,512]{1,0:T(8,128)(2,1)} all-gather(bf16[256,128]{1,0:T(8,128)(2,1)} %param.16), channel_id=1, replica_groups=mesh['walk'=2,'row'=4,'col'=4] {'col'}, dimensions={1}, use_global_device_ids=true | all-gather | bytes 327680 | tf_op jit(solution)/shard_map/all_gather | solution.py:78
  32.0 7.4 %all-gather.7.cloned.1.call-done = bf16[1024,512]{1,0:T(8,128)(2,1)} async-done(((bf16[256,512]{1,0:T(8,128)(2,1)}), bf16[1024,512]{1,0:T(8,128)(2,1)}) %all-gather.7.cloned.1.call-update) | async-done | bytes 1048592 | tf_op jit(solution)/shard_map/all_gather | solution.py:82
  42.5 132.1 %while.24 = (s32[]{:T(128)}, f32[8,32,512]{2,1,0:T(8,128)S(1)}, s32[8]{0:T(128)S(1)}, f32[256,512]{1,0:T(8,128)S(1)}, f32[256,512]{1,0:T(8,128)S(1)}, /*index=5*...) while((s32[]{:T(128)}, f32[8,32,512]{2,1,0:T(8,128)S(1)}, ...), condition=%wide.region_2.3_spmd, body=%wide.region_0.2_spmd.sunk | while | flops 4341088256 | bytes 55620052 | solution.py:39
  48.1 5.8 %multiply_convert_fusion.4 = bf16[8192,512]{1,0:T(8,128)(2,1)S(1)} fusion(f32[32,256,512]{2,1,0:T(8,128)S(1)} %add_add_fusion.4, f32[512]{0:T(512)S(1)} %copy-done.7, f32[8192]{0:T(1024)S(1)} %bitcast.107), kind=kLoop, calls=%fused_computation.3.clone.1 | loop fusion | flops 29360128 | bytes 25200640 | tf_op jit(solution)/shard_map/while/body/eval_jaxpr/convert_element_type | solution.py:31
  54.0 5.0 %bitcast_reduce_fusion.4 = f32[32,512]{1,0:T(8,128)S(1)} fusion(bf16[8192,512]{1,0:T(8,128)(2,1)S(1)} %multiply_convert_fusion.4, bf16[512,512]{1,0:T(8,128)(2,1)S(1)} %copy-done.4, f32[512]{0:T(512)S(1)} %bitcast.112), kind=kOutput, calls=%fused_computation.clone.1 | convolution fusion | flops 4303339520 | bytes 8980480 | tf_op jit(solution)/shard_map/while/body/eval_jaxpr/dot_general | solution.py:34
  64.6 5.8 %multiply_convert_fusion.4 = bf16[8192,512]{1,0:T(8,128)(2,1)S(1)} fusion(f32[32,256,512]{2,1,0:T(8,128)S(1)} %add_add_fusion.4, f32[512]{0:T(512)S(1)} %copy-done.7, f32[8192]{0:T(1024)S(1)} %bitcast.107), kind=kLoop, calls=%fused_computation.3.clone.1 | loop fusion | flops 29360128 | bytes 25200640 | tf_op jit(solution)/shard_map/while/body/eval_jaxpr/convert_element_type | solution.py:31
  70.5 5.0 %bitcast_reduce_fusion.4 = f32[32,512]{1,0:T(8,128)S(1)} fusion(bf16[8192,512]{1,0:T(8,128)(2,1)S(1)} %multiply_convert_fusion.4, bf16[512,512]{1,0:T(8,128)(2,1)S(1)} %copy-done.4, f32[512]{0:T(512)S(1)} %bitcast.112), kind=kOutput, calls=%fused_computation.clone.1 | convolution fusion | flops 4303339520 | bytes 8980480 | tf_op jit(solution)/shard_map/while/body/eval_jaxpr/dot_general | solution.py:34
  81.2 5.8 %multiply_convert_fusion.4 = bf16[8192,512]{1,0:T(8,128)(2,1)S(1)} fusion(f32[32,256,512]{2,1,0:T(8,128)S(1)} %add_add_fusion.4, f32[512]{0:T(512)S(1)} %copy-done.7, f32[8192]{0:T(1024)S(1)} %bitcast.107), kind=kLoop, calls=%fused_computation.3.clone.1 | loop fusion | flops 29360128 | bytes 25200640 | tf_op jit(solution)/shard_map/while/body/eval_jaxpr/convert_element_type | solution.py:31
  87.0 5.0 %bitcast_reduce_fusion.4 = f32[32,512]{1,0:T(8,128)S(1)} fusion(bf16[8192,512]{1,0:T(8,128)(2,1)S(1)} %multiply_convert_fusion.4, bf16[512,512]{1,0:T(8,128)(2,1)S(1)} %copy-done.4, f32[512]{0:T(512)S(1)} %bitcast.112), kind=kOutput, calls=%fused_computation.clone.1 | convolution fusion | flops 4303339520 | bytes 8980480 | tf_op jit(solution)/shard_map/while/body/eval_jaxpr/dot_general | solution.py:34
  97.7 5.8 %multiply_convert_fusion.4 = bf16[8192,512]{1,0:T(8,128)(2,1)S(1)} fusion(f32[32,256,512]{2,1,0:T(8,128)S(1)} %add_add_fusion.4, f32[512]{0:T(512)S(1)} %copy-done.7, f32[8192]{0:T(1024)S(1)} %bitcast.107), kind=kLoop, calls=%fused_computation.3.clone.1 | loop fusion | flops 29360128 | bytes 25200640 | tf_op jit(solution)/shard_map/while/body/eval_jaxpr/convert_element_type | solution.py:31
  103.5 5.0 %bitcast_reduce_fusion.4 = f32[32,512]{1,0:T(8,128)S(1)} fusion(bf16[8192,512]{1,0:T(8,128)(2,1)S(1)} %multiply_convert_fusion.4, bf16[512,512]{1,0:T(8,128)(2,1)S(1)} %copy-done.4, f32[512]{0:T(512)S(1)} %bitcast.112), kind=kOutput, calls=%fused_computation.clone.1 | convolution fusion | flops 4303339520 | bytes 8980480 | tf_op jit(solution)/shard_map/while/body/eval_jaxpr/dot_general | solution.py:34
  110.9 2.4 add_add_fusion.4
  114.2 5.8 %multiply_convert_fusion.4 = bf16[8192,512]{1,0:T(8,128)(2,1)S(1)} fusion(f32[32,256,512]{2,1,0:T(8,128)S(1)} %add_add_fusion.4, f32[512]{0:T(512)S(1)} %copy-done.7, f32[8192]{0:T(1024)S(1)} %bitcast.107), kind=kLoop, calls=%fused_computation.3.clone.1 | loop fusion | flops 29360128 | bytes 25200640 | tf_op jit(solution)/shard_map/while/body/eval_jaxpr/convert_element_type | solution.py:31
  120.0 5.0 %bitcast_reduce_fusion.4 = f32[32,512]{1,0:T(8,128)S(1)} fusion(bf16[8192,512]{1,0:T(8,128)(2,1)S(1)} %multiply_convert_fusion.4, bf16[512,512]{1,0:T(8,128)(2,1)S(1)} %copy-done.4, f32[512]{0:T(512)S(1)} %bitcast.112), kind=kOutput, calls=%fused_computation.clone.1 | convolution fusion | flops 4303339520 | bytes 8980480 | tf_op jit(solution)/shard_map/while/body/eval_jaxpr/dot_general | solution.py:34
  127.4 2.4 add_add_fusion.4
  130.7 5.8 %multiply_convert_fusion.4 = bf16[8192,512]{1,0:T(8,128)(2,1)S(1)} fusion(f32[32,256,512]{2,1,0:T(8,128)S(1)} %add_add_fusion.4, f32[512]{0:T(512)S(1)} %copy-done.7, f32[8192]{0:T(1024)S(1)} %bitcast.107), kind=kLoop, calls=%fused_computation.3.clone.1 | loop fusion | flops 29360128 | bytes 25200640 | tf_op jit(solution)/shard_map/while/body/eval_jaxpr/convert_element_type | solution.py:31
  136.5 5.0 %bitcast_reduce_fusion.4 = f32[32,512]{1,0:T(8,128)S(1)} fusion(bf16[8192,512]{1,0:T(8,128)(2,1)S(1)} %multiply_convert_fusion.4, bf16[512,512]{1,0:T(8,128)(2,1)S(1)} %copy-done.4, f32[512]{0:T(512)S(1)} %bitcast.112), kind=kOutput, calls=%fused_computation.clone.1 | convolution fusion | flops 4303339520 | bytes 8980480 | tf_op jit(solution)/shard_map/while/body/eval_jaxpr/dot_general | solution.py:34
  147.2 5.8 %multiply_convert_fusion.4 = bf16[8192,512]{1,0:T(8,128)(2,1)S(1)} fusion(f32[32,256,512]{2,1,0:T(8,128)S(1)} %add_add_fusion.4, f32[512]{0:T(512)S(1)} %copy-done.7, f32[8192]{0:T(1024)S(1)} %bitcast.107), kind=kLoop, calls=%fused_computation.3.clone.1 | loop fusion | flops 29360128 | bytes 25200640 | tf_op jit(solution)/shard_map/while/body/eval_jaxpr/convert_element_type | solution.py:31
  153.0 5.0 %bitcast_reduce_fusion.4 = f32[32,512]{1,0:T(8,128)S(1)} fusion(bf16[8192,512]{1,0:T(8,128)(2,1)S(1)} %multiply_convert_fusion.4, bf16[512,512]{1,0:T(8,128)(2,1)S(1)} %copy-done.4, f32[512]{0:T(512)S(1)} %bitcast.112), kind=kOutput, calls=%fused_computation.clone.1 | convolution fusion | flops 4303339520 | bytes 8980480 | tf_op jit(solution)/shard_map/while/body/eval_jaxpr/dot_general | solution.py:34
  163.7 5.8 %multiply_convert_fusion.4 = bf16[8192,512]{1,0:T(8,128)(2,1)S(1)} fusion(f32[32,256,512]{2,1,0:T(8,128)S(1)} %add_add_fusion.4, f32[512]{0:T(512)S(1)} %copy-done.7, f32[8192]{0:T(1024)S(1)} %bitcast.107), kind=kLoop, calls=%fused_computation.3.clone.1 | loop fusion | flops 29360128 | bytes 25200640 | tf_op jit(solution)/shard_map/while/body/eval_jaxpr/convert_element_type | solution.py:31
  169.5 5.0 %bitcast_reduce_fusion.4 = f32[32,512]{1,0:T(8,128)S(1)} fusion(bf16[8192,512]{1,0:T(8,128)(2,1)S(1)} %multiply_convert_fusion.4, bf16[512,512]{1,0:T(8,128)(2,1)S(1)} %copy-done.4, f32[512]{0:T(512)S(1)} %bitcast.112), kind=kOutput, calls=%fused_computation.clone.1 | convolution fusion | flops 4303339520 | bytes 8980480 | tf_op jit(solution)/shard_map/while/body/eval_jaxpr/dot_general | solution.py:34
  175.5 21.9 %reduce-scatter.3.cloned.1.call-done = f32[256,128]{1,0:T(8,128)} async-done(((f32[256,512]{1,0:T(8,128)}), f32[256,128]{1,0:T(8,128)}) %reduce-scatter.3.cloned.1.call-update) | async-done | bytes 131088 | tf_op jit(solution)/shard_map/reduce_scatter | solution.py:95
  198.3 13.4 %all_gather.29 = bf16[256,512]{1,0:T(8,128)(2,1)} all-gather(bf16[256,128]{1,0:T(8,128)(2,1)S(1)} %add_convert_fusion.1), channel_id=1, replica_groups=mesh['walk'=2,'row'=4,'col'=4] {'col'}, dimensions={1}, use_global_device_ids=true | all-gather | bytes 327680 | tf_op jit(solution)/shard_map/all_gather | solution.py:97
  213.4 13.7 %all-gather.9.cloned.1.call-done = bf16[1024,512]{1,0:T(8,128)(2,1)} async-done(((bf16[256,512]{1,0:T(8,128)(2,1)}), bf16[1024,512]{1,0:T(8,128)(2,1)}) %all-gather.9.cloned.1.call-update) | async-done | bytes 1048592 | tf_op jit(solution)/shard_map/all_gather | solution.py:82
  228.6 132.6 %while.25 = (s32[]{:T(128)}, f32[8,32,512]{2,1,0:T(8,128)S(1)}, s32[8]{0:T(128)S(1)}, f32[256,512]{1,0:T(8,128)S(1)}, f32[256,512]{1,0:T(8,128)S(1)}, /*index=5*...) while((s32[]{:T(128)}, f32[8,32,512]{2,1,0:T(8,128)S(1)}, ...), condition=%wide.region_6.7_spmd, body=%wide.region_4.6_spmd.sunk | while | flops 4341088256 | bytes 55620052 | solution.py:39
  234.3 5.8 %multiply_convert_fusion.5 = bf16[8192,512]{1,0:T(8,128)(2,1)S(1)} fusion(f32[32,256,512]{2,1,0:T(8,128)S(1)} %add_add_fusion.5, f32[512]{0:T(512)S(1)} %copy-done.8, f32[8192]{0:T(1024)S(1)} %bitcast.108), kind=kLoop, calls=%fused_computation.12.clone.1 | loop fusion | flops 29360128 | bytes 25200640 | tf_op jit(solution)/shard_map/while/body/eval_jaxpr/convert_element_type | solution.py:31
  240.2 5.0 %bitcast_reduce_fusion.5 = f32[32,512]{1,0:T(8,128)S(1)} fusion(bf16[8192,512]{1,0:T(8,128)(2,1)S(1)} %multiply_convert_fusion.5, bf16[512,512]{1,0:T(8,128)(2,1)S(1)} %copy-done.3, f32[512]{0:T(512)S(1)} %bitcast.111), kind=kOutput, calls=%fused_computation.9.clone.1 | convolution fusion | flops 4303339520 | bytes 8980480 | tf_op jit(solution)/shard_map/while/body/eval_jaxpr/dot_general | solution.py:34
  250.9 5.8 %multiply_convert_fusion.5 = bf16[8192,512]{1,0:T(8,128)(2,1)S(1)} fusion(f32[32,256,512]{2,1,0:T(8,128)S(1)} %add_add_fusion.5, f32[512]{0:T(512)S(1)} %copy-done.8, f32[8192]{0:T(1024)S(1)} %bitcast.108), kind=kLoop, calls=%fused_computation.12.clone.1 | loop fusion | flops 29360128 | bytes 25200640 | tf_op jit(solution)/shard_map/while/body/eval_jaxpr/convert_element_type | solution.py:31
  256.7 5.0 %bitcast_reduce_fusion.5 = f32[32,512]{1,0:T(8,128)S(1)} fusion(bf16[8192,512]{1,0:T(8,128)(2,1)S(1)} %multiply_convert_fusion.5, bf16[512,512]{1,0:T(8,128)(2,1)S(1)} %copy-done.3, f32[512]{0:T(512)S(1)} %bitcast.111), kind=kOutput, calls=%fused_computation.9.clone.1 | convolution fusion | flops 4303339520 | bytes 8980480 | tf_op jit(solution)/shard_map/while/body/eval_jaxpr/dot_general | solution.py:34
  267.5 5.8 %multiply_convert_fusion.5 = bf16[8192,512]{1,0:T(8,128)(2,1)S(1)} fusion(f32[32,256,512]{2,1,0:T(8,128)S(1)} %add_add_fusion.5, f32[512]{0:T(512)S(1)} %copy-done.8, f32[8192]{0:T(1024)S(1)} %bitcast.108), kind=kLoop, calls=%fused_computation.12.clone.1 | loop fusion | flops 29360128 | bytes 25200640 | tf_op jit(solution)/shard_map/while/body/eval_jaxpr/convert_element_type | solution.py:31
  273.3 5.0 %bitcast_reduce_fusion.5 = f32[32,512]{1,0:T(8,128)S(1)} fusion(bf16[8192,512]{1,0:T(8,128)(2,1)S(1)} %multiply_convert_fusion.5, bf16[512,512]{1,0:T(8,128)(2,1)S(1)} %copy-done.3, f32[512]{0:T(512)S(1)} %bitcast.111), kind=kOutput, calls=%fused_computation.9.clone.1 | convolution fusion | flops 4303339520 | bytes 8980480 | tf_op jit(solution)/shard_map/while/body/eval_jaxpr/dot_general | solution.py:34
  284.1 5.8 %multiply_convert_fusion.5 = bf16[8192,512]{1,0:T(8,128)(2,1)S(1)} fusion(f32[32,256,512]{2,1,0:T(8,128)S(1)} %add_add_fusion.5, f32[512]{0:T(512)S(1)} %copy-done.8, f32[8192]{0:T(1024)S(1)} %bitcast.108), kind=kLoop, calls=%fused_computation.12.clone.1 | loop fusion | flops 29360128 | bytes 25200640 | tf_op jit(solution)/shard_map/while/body/eval_jaxpr/convert_element_type | solution.py:31
  289.9 5.0 %bitcast_reduce_fusion.5 = f32[32,512]{1,0:T(8,128)S(1)} fusion(bf16[8192,512]{1,0:T(8,128)(2,1)S(1)} %multiply_convert_fusion.5, bf16[512,512]{1,0:T(8,128)(2,1)S(1)} %copy-done.3, f32[512]{0:T(512)S(1)} %bitcast.111), kind=kOutput, calls=%fused_computation.9.clone.1 | convolution fusion | flops 4303339520 | bytes 8980480 | tf_op jit(solution)/shard_map/while/body/eval_jaxpr/dot_general | solution.py:34
  300.6 5.8 %multiply_convert_fusion.5 = bf16[8192,512]{1,0:T(8,128)(2,1)S(1)} fusion(f32[32,256,512]{2,1,0:T(8,128)S(1)} %add_add_fusion.5, f32[512]{0:T(512)S(1)} %copy-done.8, f32[8192]{0:T(1024)S(1)} %bitcast.108), kind=kLoop, calls=%fused_computation.12.clone.1 | loop fusion | flops 29360128 | bytes 25200640 | tf_op jit(solution)/shard_map/while/body/eval_jaxpr/convert_element_type | solution.py:31
  306.5 5.0 %bitcast_reduce_fusion.5 = f32[32,512]{1,0:T(8,128)S(1)} fusion(bf16[8192,512]{1,0:T(8,128)(2,1)S(1)} %multiply_convert_fusion.5, bf16[512,512]{1,0:T(8,128)(2,1)S(1)} %copy-done.3, f32[512]{0:T(512)S(1)} %bitcast.111), kind=kOutput, calls=%fused_computation.9.clone.1 | convolution fusion | flops 4303339520 | bytes 8980480 | tf_op jit(solution)/shard_map/while/body/eval_jaxpr/dot_general | solution.py:34
  317.2 5.8 %multiply_convert_fusion.5 = bf16[8192,512]{1,0:T(8,128)(2,1)S(1)} fusion(f32[32,256,512]{2,1,0:T(8,128)S(1)} %add_add_fusion.5, f32[512]{0:T(512)S(1)} %copy-done.8, f32[8192]{0:T(1024)S(1)} %bitcast.108), kind=kLoop, calls=%fused_computation.12.clone.1 | loop fusion | flops 29360128 | bytes 25200640 | tf_op jit(solution)/shard_map/while/body/eval_jaxpr/convert_element_type | solution.py:31
  323.1 5.0 %bitcast_reduce_fusion.5 = f32[32,512]{1,0:T(8,128)S(1)} fusion(bf16[8192,512]{1,0:T(8,128)(2,1)S(1)} %multiply_convert_fusion.5, bf16[512,512]{1,0:T(8,128)(2,1)S(1)} %copy-done.3, f32[512]{0:T(512)S(1)} %bitcast.111), kind=kOutput, calls=%fused_computation.9.clone.1 | convolution fusion | flops 4303339520 | bytes 8980480 | tf_op jit(solution)/shard_map/while/body/eval_jaxpr/dot_general | solution.py:34
  333.8 5.8 %multiply_convert_fusion.5 = bf16[8192,512]{1,0:T(8,128)(2,1)S(1)} fusion(f32[32,256,512]{2,1,0:T(8,128)S(1)} %add_add_fusion.5, f32[512]{0:T(512)S(1)} %copy-done.8, f32[8192]{0:T(1024)S(1)} %bitcast.108), kind=kLoop, calls=%fused_computation.12.clone.1 | loop fusion | flops 29360128 | bytes 25200640 | tf_op jit(solution)/shard_map/while/body/eval_jaxpr/convert_element_type | solution.py:31
  339.6 5.0 %bitcast_reduce_fusion.5 = f32[32,512]{1,0:T(8,128)S(1)} fusion(bf16[8192,512]{1,0:T(8,128)(2,1)S(1)} %multiply_convert_fusion.5, bf16[512,512]{1,0:T(8,128)(2,1)S(1)} %copy-done.3, f32[512]{0:T(512)S(1)} %bitcast.111), kind=kOutput, calls=%fused_computation.9.clone.1 | convolution fusion | flops 4303339520 | bytes 8980480 | tf_op jit(solution)/shard_map/while/body/eval_jaxpr/dot_general | solution.py:34
  350.4 5.8 %multiply_convert_fusion.5 = bf16[8192,512]{1,0:T(8,128)(2,1)S(1)} fusion(f32[32,256,512]{2,1,0:T(8,128)S(1)} %add_add_fusion.5, f32[512]{0:T(512)S(1)} %copy-done.8, f32[8192]{0:T(1024)S(1)} %bitcast.108), kind=kLoop, calls=%fused_computation.12.clone.1 | loop fusion | flops 29360128 | bytes 25200640 | tf_op jit(solution)/shard_map/while/body/eval_jaxpr/convert_element_type | solution.py:31
  356.2 5.0 %bitcast_reduce_fusion.5 = f32[32,512]{1,0:T(8,128)S(1)} fusion(bf16[8192,512]{1,0:T(8,128)(2,1)S(1)} %multiply_convert_fusion.5, bf16[512,512]{1,0:T(8,128)(2,1)S(1)} %copy-done.3, f32[512]{0:T(512)S(1)} %bitcast.111), kind=kOutput, calls=%fused_computation.9.clone.1 | convolution fusion | flops 4303339520 | bytes 8980480 | tf_op jit(solution)/shard_map/while/body/eval_jaxpr/dot_general | solution.py:34
  362.7 21.3 %reduce-scatter.5.cloned.1.call-done = f32[256,128]{1,0:T(8,128)} async-done(((f32[256,512]{1,0:T(8,128)}), f32[256,128]{1,0:T(8,128)}) %reduce-scatter.5.cloned.1.call-update) | async-done | bytes 131088 | tf_op jit(solution)/shard_map/reduce_scatter | solution.py:95
  385.0 12.8 %all_gather.31 = bf16[256,512]{1,0:T(8,128)(2,1)S(1)} all-gather(bf16[256,128]{1,0:T(8,128)(2,1)S(1)} %add_convert_fusion), channel_id=1, replica_groups=mesh['walk'=2,'row'=4,'col'=4] {'col'}, dimensions={1}, use_global_device_ids=true | all-gather | bytes 327680 | tf_op jit(solution)/shard_map/all_gather | solution.py:97
  400.6 29.9 %all-gather.11.cloned.1.call-done = f32[256,1024]{1,0:T(8,128)} async-done(((f32[256,256]{1,0:T(8,128)}), f32[256,1024]{1,0:T(8,128)}) %all-gather.11.cloned.1.call-update) | async-done | bytes 1048592 | tf_op jit(solution)/shard_map/all_gather | solution.py:99
  430.5 3.3 convolution_subtract_fusion
  433.8 25.7 %all-gather.17.cloned.1.call-done = f32[256,1024]{1,0:T(8,128)} async-done(((f32[256,256]{1,0:T(8,128)}), f32[256,1024]{1,0:T(8,128)}) %all-gather.17.cloned.1.call-update) | async-done | bytes 1048592 | tf_op jit(solution)/shard_map/all_gather | solution.py:111
  459.5 18.2 %all-gather.15.cloned.1.call-done = f32[1024,256]{1,0:T(8,128)} async-done(((f32[256,256]{1,0:T(8,128)}), f32[1024,256]{1,0:T(8,128)}) %all-gather.15.cloned.1.call-update) | async-done | bytes 1048592 | tf_op jit(solution)/shard_map/all_gather | solution.py:115
  477.7 3.4 convolution_bitcast_fusion
  (221 shorter events, 96.8 us)
Async XLA Ops:
  7.2 390.7 %copy-start = (bf16[512,256]{1,0:T(8,128)(2,1)S(1)}, bf16[512,256]{1,0:T(8,128)(2,1)}, u32[]{:S(2)}) copy-start(bf16[512,256]{1,0:T(8,128)(2,1)} %param.25) | copy-start | bytes 786436
  7.2 32.2 %all-gather.7.cloned.1.call-start = ((), (), s32[]{:S(2)}) async-start(), calls=%async_computation.2 | async-start | bytes 1310720 | tf_op jit(solution)/shard_map/all_gather | solution.py:82
  23.9 173.5 %reduce-scatter.3.cloned.1.call-start = ((), (), s32[]{:S(2)}) async-start(), calls=%async_computation.3 | async-start | bytes 655360 | tf_op jit(solution)/shard_map/reduce_scatter | solution.py:95
  42.5 154.9 %copy-start.5 = (bf16[256,128]{1,0:T(8,128)(2,1)S(1)}, bf16[256,128]{1,0:T(8,128)(2,1)}, u32[]{:S(2)}) copy-start(bf16[256,128]{1,0:T(8,128)(2,1)} %param.16) | copy-start | bytes 196612
  42.5 5.6 %copy-start.7 = (f32[512]{0:T(512)S(1)}, f32[512]{0:T(512)}, u32[]{:S(2)}) copy-start(f32[512]{0:T(512)} %get-tuple-element.471) | copy-start | bytes 6148 | tf_op jit(solution)/shard_map/while
  47.3 6.7 %copy-start.4 = (bf16[512,512]{1,0:T(8,128)(2,1)S(1)}, bf16[512,512]{1,0:T(8,128)(2,1)}, u32[]{:S(2)}) copy-start(bf16[512,512]{1,0:T(8,128)(2,1)} %get-tuple-element.472) | copy-start | bytes 1572868 | tf_op jit(solution)/shard_map/while
  59.0 5.6 %copy-start.7 = (f32[512]{0:T(512)S(1)}, f32[512]{0:T(512)}, u32[]{:S(2)}) copy-start(f32[512]{0:T(512)} %get-tuple-element.471) | copy-start | bytes 6148 | tf_op jit(solution)/shard_map/while
  63.8 6.7 %copy-start.4 = (bf16[512,512]{1,0:T(8,128)(2,1)S(1)}, bf16[512,512]{1,0:T(8,128)(2,1)}, u32[]{:S(2)}) copy-start(bf16[512,512]{1,0:T(8,128)(2,1)} %get-tuple-element.472) | copy-start | bytes 1572868 | tf_op jit(solution)/shard_map/while
  75.6 5.6 %copy-start.7 = (f32[512]{0:T(512)S(1)}, f32[512]{0:T(512)}, u32[]{:S(2)}) copy-start(f32[512]{0:T(512)} %get-tuple-element.471) | copy-start | bytes 6148 | tf_op jit(solution)/shard_map/while
  80.3 6.7 %copy-start.4 = (bf16[512,512]{1,0:T(8,128)(2,1)S(1)}, bf16[512,512]{1,0:T(8,128)(2,1)}, u32[]{:S(2)}) copy-start(bf16[512,512]{1,0:T(8,128)(2,1)} %get-tuple-element.472) | copy-start | bytes 1572868 | tf_op jit(solution)/shard_map/while
  92.1 5.6 %copy-start.7 = (f32[512]{0:T(512)S(1)}, f32[512]{0:T(512)}, u32[]{:S(2)}) copy-start(f32[512]{0:T(512)} %get-tuple-element.471) | copy-start | bytes 6148 | tf_op jit(solution)/shard_map/while
  96.8 6.7 %copy-start.4 = (bf16[512,512]{1,0:T(8,128)(2,1)S(1)}, bf16[512,512]{1,0:T(8,128)(2,1)}, u32[]{:S(2)}) copy-start(bf16[512,512]{1,0:T(8,128)(2,1)} %get-tuple-element.472) | copy-start | bytes 1572868 | tf_op jit(solution)/shard_map/while
  108.6 5.6 %copy-start.7 = (f32[512]{0:T(512)S(1)}, f32[512]{0:T(512)}, u32[]{:S(2)}) copy-start(f32[512]{0:T(512)} %get-tuple-element.471) | copy-start | bytes 6148 | tf_op jit(solution)/shard_map/while
  113.3 6.7 %copy-start.4 = (bf16[512,512]{1,0:T(8,128)(2,1)S(1)}, bf16[512,512]{1,0:T(8,128)(2,1)}, u32[]{:S(2)}) copy-start(bf16[512,512]{1,0:T(8,128)(2,1)} %get-tuple-element.472) | copy-start | bytes 1572868 | tf_op jit(solution)/shard_map/while
  125.1 5.6 %copy-start.7 = (f32[512]{0:T(512)S(1)}, f32[512]{0:T(512)}, u32[]{:S(2)}) copy-start(f32[512]{0:T(512)} %get-tuple-element.471) | copy-start | bytes 6148 | tf_op jit(solution)/shard_map/while
  129.8 6.7 %copy-start.4 = (bf16[512,512]{1,0:T(8,128)(2,1)S(1)}, bf16[512,512]{1,0:T(8,128)(2,1)}, u32[]{:S(2)}) copy-start(bf16[512,512]{1,0:T(8,128)(2,1)} %get-tuple-element.472) | copy-start | bytes 1572868 | tf_op jit(solution)/shard_map/while
  141.6 5.6 %copy-start.7 = (f32[512]{0:T(512)S(1)}, f32[512]{0:T(512)}, u32[]{:S(2)}) copy-start(f32[512]{0:T(512)} %get-tuple-element.471) | copy-start | bytes 6148 | tf_op jit(solution)/shard_map/while
  146.3 6.7 %copy-start.4 = (bf16[512,512]{1,0:T(8,128)(2,1)S(1)}, bf16[512,512]{1,0:T(8,128)(2,1)}, u32[]{:S(2)}) copy-start(bf16[512,512]{1,0:T(8,128)(2,1)} %get-tuple-element.472) | copy-start | bytes 1572868 | tf_op jit(solution)/shard_map/while
  158.1 5.6 %copy-start.7 = (f32[512]{0:T(512)S(1)}, f32[512]{0:T(512)}, u32[]{:S(2)}) copy-start(f32[512]{0:T(512)} %get-tuple-element.471) | copy-start | bytes 6148 | tf_op jit(solution)/shard_map/while
  162.8 6.7 %copy-start.4 = (bf16[512,512]{1,0:T(8,128)(2,1)S(1)}, bf16[512,512]{1,0:T(8,128)(2,1)}, u32[]{:S(2)}) copy-start(bf16[512,512]{1,0:T(8,128)(2,1)} %get-tuple-element.472) | copy-start | bytes 1572868 | tf_op jit(solution)/shard_map/while
  174.6 0.8 copy-start.2
  175.4 51.7 %all-gather.9.cloned.1.call-start = ((), (), s32[]{:S(2)}) async-start(), calls=%async_computation.4 | async-start | bytes 1310720 | tf_op jit(solution)/shard_map/all_gather | solution.py:82
  211.8 172.3 %reduce-scatter.5.cloned.1.call-start = ((), (), s32[]{:S(2)}) async-start(), calls=%async_computation.5 | async-start | bytes 655360 | tf_op jit(solution)/shard_map/reduce_scatter | solution.py:95
  228.6 5.7 %copy-start.8 = (f32[512]{0:T(512)S(1)}, f32[512]{0:T(512)}, u32[]{:S(2)}) copy-start(f32[512]{0:T(512)} %get-tuple-element.525) | copy-start | bytes 6148 | tf_op jit(solution)/shard_map/while
  233.4 6.7 %copy-start.3 = (bf16[512,512]{1,0:T(8,128)(2,1)S(1)}, bf16[512,512]{1,0:T(8,128)(2,1)}, u32[]{:S(2)}) copy-start(bf16[512,512]{1,0:T(8,128)(2,1)} %get-tuple-element.526) | copy-start | bytes 1572868 | tf_op jit(solution)/shard_map/while
  245.2 5.7 %copy-start.8 = (f32[512]{0:T(512)S(1)}, f32[512]{0:T(512)}, u32[]{:S(2)}) copy-start(f32[512]{0:T(512)} %get-tuple-element.525) | copy-start | bytes 6148 | tf_op jit(solution)/shard_map/while
  250.0 6.7 %copy-start.3 = (bf16[512,512]{1,0:T(8,128)(2,1)S(1)}, bf16[512,512]{1,0:T(8,128)(2,1)}, u32[]{:S(2)}) copy-start(bf16[512,512]{1,0:T(8,128)(2,1)} %get-tuple-element.526) | copy-start | bytes 1572868 | tf_op jit(solution)/shard_map/while
  261.8 5.7 %copy-start.8 = (f32[512]{0:T(512)S(1)}, f32[512]{0:T(512)}, u32[]{:S(2)}) copy-start(f32[512]{0:T(512)} %get-tuple-element.525) | copy-start | bytes 6148 | tf_op jit(solution)/shard_map/while
  266.6 6.7 %copy-start.3 = (bf16[512,512]{1,0:T(8,128)(2,1)S(1)}, bf16[512,512]{1,0:T(8,128)(2,1)}, u32[]{:S(2)}) copy-start(bf16[512,512]{1,0:T(8,128)(2,1)} %get-tuple-element.526) | copy-start | bytes 1572868 | tf_op jit(solution)/shard_map/while
  278.4 5.7 %copy-start.8 = (f32[512]{0:T(512)S(1)}, f32[512]{0:T(512)}, u32[]{:S(2)}) copy-start(f32[512]{0:T(512)} %get-tuple-element.525) | copy-start | bytes 6148 | tf_op jit(solution)/shard_map/while
  283.2 6.7 %copy-start.3 = (bf16[512,512]{1,0:T(8,128)(2,1)S(1)}, bf16[512,512]{1,0:T(8,128)(2,1)}, u32[]{:S(2)}) copy-start(bf16[512,512]{1,0:T(8,128)(2,1)} %get-tuple-element.526) | copy-start | bytes 1572868 | tf_op jit(solution)/shard_map/while
  295.0 5.7 %copy-start.8 = (f32[512]{0:T(512)S(1)}, f32[512]{0:T(512)}, u32[]{:S(2)}) copy-start(f32[512]{0:T(512)} %get-tuple-element.525) | copy-start | bytes 6148 | tf_op jit(solution)/shard_map/while
  299.8 6.7 %copy-start.3 = (bf16[512,512]{1,0:T(8,128)(2,1)S(1)}, bf16[512,512]{1,0:T(8,128)(2,1)}, u32[]{:S(2)}) copy-start(bf16[512,512]{1,0:T(8,128)(2,1)} %get-tuple-element.526) | copy-start | bytes 1572868 | tf_op jit(solution)/shard_map/while
  311.5 5.7 %copy-start.8 = (f32[512]{0:T(512)S(1)}, f32[512]{0:T(512)}, u32[]{:S(2)}) copy-start(f32[512]{0:T(512)} %get-tuple-element.525) | copy-start | bytes 6148 | tf_op jit(solution)/shard_map/while
  316.4 6.7 %copy-start.3 = (bf16[512,512]{1,0:T(8,128)(2,1)S(1)}, bf16[512,512]{1,0:T(8,128)(2,1)}, u32[]{:S(2)}) copy-start(bf16[512,512]{1,0:T(8,128)(2,1)} %get-tuple-element.526) | copy-start | bytes 1572868 | tf_op jit(solution)/shard_map/while
  328.1 5.7 %copy-start.8 = (f32[512]{0:T(512)S(1)}, f32[512]{0:T(512)}, u32[]{:S(2)}) copy-start(f32[512]{0:T(512)} %get-tuple-element.525) | copy-start | bytes 6148 | tf_op jit(solution)/shard_map/while
  332.9 6.7 %copy-start.3 = (bf16[512,512]{1,0:T(8,128)(2,1)S(1)}, bf16[512,512]{1,0:T(8,128)(2,1)}, u32[]{:S(2)}) copy-start(bf16[512,512]{1,0:T(8,128)(2,1)} %get-tuple-element.526) | copy-start | bytes 1572868 | tf_op jit(solution)/shard_map/while
  344.7 5.7 %copy-start.8 = (f32[512]{0:T(512)S(1)}, f32[512]{0:T(512)}, u32[]{:S(2)}) copy-start(f32[512]{0:T(512)} %get-tuple-element.525) | copy-start | bytes 6148 | tf_op jit(solution)/shard_map/while
  349.5 6.7 %copy-start.3 = (bf16[512,512]{1,0:T(8,128)(2,1)S(1)}, bf16[512,512]{1,0:T(8,128)(2,1)}, u32[]{:S(2)}) copy-start(bf16[512,512]{1,0:T(8,128)(2,1)} %get-tuple-element.526) | copy-start | bytes 1572868 | tf_op jit(solution)/shard_map/while
  361.3 0.8 copy-start.1
  362.1 38.5 %all-gather.13.cloned.1.call-start = ((), (), s32[]{:S(2)}) async-start(), calls=%async_computation.7 | async-start | bytes 1310720 | tf_op jit(solution)/shard_map/all_gather | solution.py:103
  362.7 67.8 %all-gather.11.cloned.1.call-start = ((), (), s32[]{:S(2)}) async-start(), calls=%async_computation.6 | async-start | bytes 1310720 | tf_op jit(solution)/shard_map/all_gather | solution.py:99
  385.0 96.9 %copy-start.6 = (bf16[256,128]{1,0:T(8,128)(2,1)}, bf16[256,128]{1,0:T(8,128)(2,1)S(1)}, u32[]{:S(2)}) copy-start(bf16[256,128]{1,0:T(8,128)(2,1)S(1)} %add_convert_fusion) | copy-start | bytes 196612
  399.7 59.7 %all-gather.17.cloned.1.call-start = ((), (), s32[]{:S(2)}) async-start(), calls=%async_computation.9 | async-start | bytes 1310720 | tf_op jit(solution)/shard_map/all_gather | solution.py:111
  400.5 77.2 %all-gather.15.cloned.1.call-start = ((), (), s32[]{:S(2)}) async-start(), calls=%async_computation.8 | async-start | bytes 1310720 | tf_op jit(solution)/shard_map/all_gather | solution.py:115
Sparse Core Ops, SparseCore 0:
  24.0 15.3 all-gather.6
  175.5 21.8 reduce-scatter.2
  211.9 15.1 all-gather.8
  362.2 21.8 reduce-scatter.4
  385.5 14.9 all-gather.12
  402.5 27.9 all-gather.10
  432.1 27.3 all-gather.16
  461.6 16.0 all-gather.14
where the time goes:
time: 491 us; the launch traced here: 489 us
  waiting for transfers between devices  140 us (29%)
  other arithmetic  134 us (27%)
  matrix products  95.6 us (19%)
  local copies, waits for them, and re-layouts  49.9 us (10%)
  blocking collectives  42.9 us (9%)
  between operations  14.3 us (3%)
  loops' own time  11.7 us (2%)
    convert_element_type x16, other arithmetic, one_step(): gated_vals = jax.nn.silu(pre_act).astype(jnp.bfloat16)  93.1 us
    dot_general x16, matrix products, one_step(): jnp.dot(flat_rows, weight_out, preferred_element_type=jnp.float32)  80.4 us
    reduce_scatter x2, waiting for transfers between devices, per_device(): lax.psum_scatter(pair_sums, 'col', scatter_dimension=1, tiled=True) / N  43.3 us
    add x16, other arithmetic, one_step(): left_rows[:, None, :] + right_part[None, :, :] + shift_rows[None, :, :]  38.6 us
    all_gather x1, waiting for transfers between devices, per_device(): panel = lax.all_gather(orbital, 'col', axis=1, tiled=True)  29.9 us
    all_gather x2, blocking collectives, per_device(): full_rows = lax.all_gather(own_shard, 'col', axis=1, tiled=True)  26.2 us
    all_gather x1, waiting for transfers between devices, per_device(): inverse_panel = lax.all_gather(approx_inverse, 'col', axis=1, tiled=True)  25.7 us
    all_gather x2, waiting for transfers between devices, per_device(): gathered = lax.all_gather(full_rows, 'row', axis=0, tiled=True)  21.1 us
  transfers between devices with their start and end apart: 8, of which 7 were waited for; matrix products, arithmetic and copies ran while one was open for 3% of the time, Pallas kernels for 0%

commit v1 on v0

--- a/solution.py
+++ b/solution.py
@@ -96,7 +96,12 @@
         own_shard = (own_shard.astype(jnp.float32) + shares).astype(jnp.bfloat16)
         full_rows = lax.all_gather(own_shard, "col", axis=1, tiled=True)
     orbital = jnp.dot(full_rows, w_orbital, preferred_element_type=jnp.float32) * envelope
-    panel = lax.all_gather(orbital, "col", axis=1, tiled=True)
+    ring = [orbital]
+    for hop in range(3):
+        ring.append(lax.ppermute(ring[-1], "col", [(dev, (dev + 1) % 4) for dev in range(4)]))
+    panel = jnp.roll(
+        jnp.concatenate(ring[::-1], axis=1), (lax.axis_index("col") + 1) * ring[0].shape[1], axis=1
+    )
     left_cols = panel
     product = jnp.dot(
         left_cols,

time: 491 us -> 471 us (0.959)
  waiting for transfers between devices: 140 us -> 120 us
    ppermute x0 -> x3, waiting for transfers between devices: none -> 33.5 us  [per_device(): lax.ppermute(ring[-1], 'col', [(dev, (dev + 1) % 4) for dev in range(4)])]
    all_gather x1 -> x0, waiting for transfers between devices: 29.9 us -> none  [per_device(): panel = lax.all_gather(orbital, 'col', axis=1, tiled=True)]
    all_gather x1, waiting for transfers between devices: 25.7 us -> 3.87 us  [per_device(): inverse_panel = lax.all_gather(approx_inverse, 'col', axis=1, tiled=True)]
  transfers between devices with their start and end apart: 8 -> 10, of which waited for: 7 -> 9; matrix products, arithmetic and copies ran while one was open for 3% -> 3% of each run, Pallas kernels for 0% -> 0%
where the time goes in v1:
time: 471 us; the launch traced here: 469 us
  other arithmetic  134 us (28%)
  waiting for transfers between devices  120 us (25%)
  matrix products  94.5 us (20%)
  local copies, waits for them, and re-layouts  51.2 us (11%)
  blocking collectives  42.9 us (9%)
  between operations  14.4 us (3%)
  loops' own time  11.7 us (2%)
    convert_element_type x16, other arithmetic, one_step(): gated_vals = jax.nn.silu(pre_act).astype(jnp.bfloat16)  93.1 us
    dot_general x16, matrix products, one_step(): jnp.dot(flat_rows, weight_out, preferred_element_type=jnp.float32)  80.4 us
    reduce_scatter x2, waiting for transfers between devices, per_device(): lax.psum_scatter(pair_sums, 'col', scatter_dimension=1, tiled=True) / N  42.2 us
    add x16, other arithmetic, one_step(): left_rows[:, None, :] + right_part[None, :, :] + shift_rows[None, :, :]  38.6 us
    ppermute x3, waiting for transfers between devices, per_device(): lax.ppermute(ring[-1], 'col', [(dev, (dev + 1) % 4) for dev in range(4)])  33.5 us
    all_gather x2, blocking collectives, per_device(): full_rows = lax.all_gather(own_shard, 'col', axis=1, tiled=True)  26.2 us
    all_gather x2, waiting for transfers between devices, per_device(): gathered = lax.all_gather(full_rows, 'row', axis=0, tiled=True)  21.1 us
    all_gather x1, waiting for transfers between devices, per_device(): lax.all_gather(residual_part, 'row', axis=0, tiled=True)  18.2 us
  transfers between devices with their start and end apart: 10, of which 9 were waited for; matrix products, arithmetic and copies ran while one was open for 3% of the time, Pallas kernels for 0%

profile of v1, /device:TPU:0, one launch (start us, length us, event | category | flops | bytes accessed | tf_op | source)
XLA Modules:
  0.0 469.0 jit_solution(5269232274691497712)
XLA Ops:
  7.2 16.7 %all_gather.24 = bf16[256,512]{1,0:T(8,128)(2,1)} all-gather(bf16[256,128]{1,0:T(8,128)(2,1)} %param.16), channel_id=1, replica_groups=mesh['walk'=2,'row'=4,'col'=4] {'col'}, dimensions={1}, use_global_device_ids=true | all-gather | bytes 327680 | tf_op jit(solution)/shard_map/all_gather | solution.py:78
  32.0 7.4 %all-gather.6.cloned.1.call-done = bf16[1024,512]{1,0:T(8,128)(2,1)} async-done(((bf16[256,512]{1,0:T(8,128)(2,1)}), bf16[1024,512]{1,0:T(8,128)(2,1)}) %all-gather.6.cloned.1.call-update) | async-done | bytes 1048592 | tf_op jit(solution)/shard_map/all_gather | solution.py:82
  42.5 132.1 %while.24 = (s32[]{:T(128)}, f32[8,32,512]{2,1,0:T(8,128)S(1)}, s32[8]{0:T(128)S(1)}, f32[256,512]{1,0:T(8,128)S(1)}, f32[256,512]{1,0:T(8,128)S(1)}, /*index=5*...) while((s32[]{:T(128)}, f32[8,32,512]{2,1,0:T(8,128)S(1)}, ...), condition=%wide.region_2.3_spmd, body=%wide.region_0.2_spmd.sunk | while | flops 4341088256 | bytes 55620052 | solution.py:39
  48.1 5.8 %multiply_convert_fusion.4 = bf16[8192,512]{1,0:T(8,128)(2,1)S(1)} fusion(f32[32,256,512]{2,1,0:T(8,128)S(1)} %add_add_fusion.4, f32[512]{0:T(512)S(1)} %copy-done.7, f32[8192]{0:T(1024)S(1)} %bitcast.106), kind=kLoop, calls=%fused_computation.3.clone.1 | loop fusion | flops 29360128 | bytes 25200640 | tf_op jit(solution)/shard_map/while/body/eval_jaxpr/convert_element_type | solution.py:31
  54.0 5.0 %bitcast_reduce_fusion.4 = f32[32,512]{1,0:T(8,128)S(1)} fusion(bf16[8192,512]{1,0:T(8,128)(2,1)S(1)} %multiply_convert_fusion.4, bf16[512,512]{1,0:T(8,128)(2,1)S(1)} %copy-done.4, f32[512]{0:T(512)S(1)} %bitcast.111), kind=kOutput, calls=%fused_computation.clone.1 | convolution fusion | flops 4303339520 | bytes 8980480 | tf_op jit(solution)/shard_map/while/body/eval_jaxpr/dot_general | solution.py:34
  64.6 5.8 %multiply_convert_fusion.4 = bf16[8192,512]{1,0:T(8,128)(2,1)S(1)} fusion(f32[32,256,512]{2,1,0:T(8,128)S(1)} %add_add_fusion.4, f32[512]{0:T(512)S(1)} %copy-done.7, f32[8192]{0:T(1024)S(1)} %bitcast.106), kind=kLoop, calls=%fused_computation.3.clone.1 | loop fusion | flops 29360128 | bytes 25200640 | tf_op jit(solution)/shard_map/while/body/eval_jaxpr/convert_element_type | solution.py:31
  70.5 5.0 %bitcast_reduce_fusion.4 = f32[32,512]{1,0:T(8,128)S(1)} fusion(bf16[8192,512]{1,0:T(8,128)(2,1)S(1)} %multiply_convert_fusion.4, bf16[512,512]{1,0:T(8,128)(2,1)S(1)} %copy-done.4, f32[512]{0:T(512)S(1)} %bitcast.111), kind=kOutput, calls=%fused_computation.clone.1 | convolution fusion | flops 4303339520 | bytes 8980480 | tf_op jit(solution)/shard_map/while/body/eval_jaxpr/dot_general | solution.py:34
  81.2 5.8 %multiply_convert_fusion.4 = bf16[8192,512]{1,0:T(8,128)(2,1)S(1)} fusion(f32[32,256,512]{2,1,0:T(8,128)S(1)} %add_add_fusion.4, f32[512]{0:T(512)S(1)} %copy-done.7, f32[8192]{0:T(1024)S(1)} %bitcast.106), kind=kLoop, calls=%fused_computation.3.clone.1 | loop fusion | flops 29360128 | bytes 25200640 | tf_op jit(solution)/shard_map/while/body/eval_jaxpr/convert_element_type | solution.py:31
  87.0 5.0 %bitcast_reduce_fusion.4 = f32[32,512]{1,0:T(8,128)S(1)} fusion(bf16[8192,512]{1,0:T(8,128)(2,1)S(1)} %multiply_convert_fusion.4, bf16[512,512]{1,0:T(8,128)(2,1)S(1)} %copy-done.4, f32[512]{0:T(512)S(1)} %bitcast.111), kind=kOutput, calls=%fused_computation.clone.1 | convolution fusion | flops 4303339520 | bytes 8980480 | tf_op jit(solution)/shard_map/while/body/eval_jaxpr/dot_general | solution.py:34
  97.7 5.8 %multiply_convert_fusion.4 = bf16[8192,512]{1,0:T(8,128)(2,1)S(1)} fusion(f32[32,256,512]{2,1,0:T(8,128)S(1)} %add_add_fusion.4, f32[512]{0:T(512)S(1)} %copy-done.7, f32[8192]{0:T(1024)S(1)} %bitcast.106), kind=kLoop, calls=%fused_computation.3.clone.1 | loop fusion | flops 29360128 | bytes 25200640 | tf_op jit(solution)/shard_map/while/body/eval_jaxpr/convert_element_type | solution.py:31
  103.5 5.0 %bitcast_reduce_fusion.4 = f32[32,512]{1,0:T(8,128)S(1)} fusion(bf16[8192,512]{1,0:T(8,128)(2,1)S(1)} %multiply_convert_fusion.4, bf16[512,512]{1,0:T(8,128)(2,1)S(1)} %copy-done.4, f32[512]{0:T(512)S(1)} %bitcast.111), kind=kOutput, calls=%fused_computation.clone.1 | convolution fusion | flops 4303339520 | bytes 8980480 | tf_op jit(solution)/shard_map/while/body/eval_jaxpr/dot_general | solution.py:34
  114.2 5.8 %multiply_convert_fusion.4 = bf16[8192,512]{1,0:T(8,128)(2,1)S(1)} fusion(f32[32,256,512]{2,1,0:T(8,128)S(1)} %add_add_fusion.4, f32[512]{0:T(512)S(1)} %copy-done.7, f32[8192]{0:T(1024)S(1)} %bitcast.106), kind=kLoop, calls=%fused_computation.3.clone.1 | loop fusion | flops 29360128 | bytes 25200640 | tf_op jit(solution)/shard_map/while/body/eval_jaxpr/convert_element_type | solution.py:31
  120.0 5.0 %bitcast_reduce_fusion.4 = f32[32,512]{1,0:T(8,128)S(1)} fusion(bf16[8192,512]{1,0:T(8,128)(2,1)S(1)} %multiply_convert_fusion.4, bf16[512,512]{1,0:T(8,128)(2,1)S(1)} %copy-done.4, f32[512]{0:T(512)S(1)} %bitcast.111), kind=kOutput, calls=%fused_computation.clone.1 | convolution fusion | flops 4303339520 | bytes 8980480 | tf_op jit(solution)/shard_map/while/body/eval_jaxpr/dot_general | solution.py:34
  130.7 5.8 %multiply_convert_fusion.4 = bf16[8192,512]{1,0:T(8,128)(2,1)S(1)} fusion(f32[32,256,512]{2,1,0:T(8,128)S(1)} %add_add_fusion.4, f32[512]{0:T(512)S(1)} %copy-done.7, f32[8192]{0:T(1024)S(1)} %bitcast.106), kind=kLoop, calls=%fused_computation.3.clone.1 | loop fusion | flops 29360128 | bytes 25200640 | tf_op jit(solution)/shard_map/while/body/eval_jaxpr/convert_element_type | solution.py:31
  136.5 5.0 %bitcast_reduce_fusion.4 = f32[32,512]{1,0:T(8,128)S(1)} fusion(bf16[8192,512]{1,0:T(8,128)(2,1)S(1)} %multiply_convert_fusion.4, bf16[512,512]{1,0:T(8,128)(2,1)S(1)} %copy-done.4, f32[512]{0:T(512)S(1)} %bitcast.111), kind=kOutput, calls=%fused_computation.clone.1 | convolution fusion | flops 4303339520 | bytes 8980480 | tf_op jit(solution)/shard_map/while/body/eval_jaxpr/dot_general | solution.py:34
  147.2 5.8 %multiply_convert_fusion.4 = bf16[8192,512]{1,0:T(8,128)(2,1)S(1)} fusion(f32[32,256,512]{2,1,0:T(8,128)S(1)} %add_add_fusion.4, f32[512]{0:T(512)S(1)} %copy-done.7, f32[8192]{0:T(1024)S(1)} %bitcast.106), kind=kLoop, calls=%fused_computation.3.clone.1 | loop fusion | flops 29360128 | bytes 25200640 | tf_op jit(solution)/shard_map/while/body/eval_jaxpr/convert_element_type | solution.py:31
  153.0 5.0 %bitcast_reduce_fusion.4 = f32[32,512]{1,0:T(8,128)S(1)} fusion(bf16[8192,512]{1,0:T(8,128)(2,1)S(1)} %multiply_convert_fusion.4, bf16[512,512]{1,0:T(8,128)(2,1)S(1)} %copy-done.4, f32[512]{0:T(512)S(1)} %bitcast.111), kind=kOutput, calls=%fused_computation.clone.1 | convolution fusion | flops 4303339520 | bytes 8980480 | tf_op jit(solution)/shard_map/while/body/eval_jaxpr/dot_general | solution.py:34
  163.7 5.8 %multiply_convert_fusion.4 = bf16[8192,512]{1,0:T(8,128)(2,1)S(1)} fusion(f32[32,256,512]{2,1,0:T(8,128)S(1)} %add_add_fusion.4, f32[512]{0:T(512)S(1)} %copy-done.7, f32[8192]{0:T(1024)S(1)} %bitcast.106), kind=kLoop, calls=%fused_computation.3.clone.1 | loop fusion | flops 29360128 | bytes 25200640 | tf_op jit(solution)/shard_map/while/body/eval_jaxpr/convert_element_type | solution.py:31
  169.5 5.0 %bitcast_reduce_fusion.4 = f32[32,512]{1,0:T(8,128)S(1)} fusion(bf16[8192,512]{1,0:T(8,128)(2,1)S(1)} %multiply_convert_fusion.4, bf16[512,512]{1,0:T(8,128)(2,1)S(1)} %copy-done.4, f32[512]{0:T(512)S(1)} %bitcast.111), kind=kOutput, calls=%fused_computation.clone.1 | convolution fusion | flops 4303339520 | bytes 8980480 | tf_op jit(solution)/shard_map/while/body/eval_jaxpr/dot_general | solution.py:34
  175.5 21.9 %reduce-scatter.3.cloned.1.call-done = f32[256,128]{1,0:T(8,128)} async-done(((f32[256,512]{1,0:T(8,128)}), f32[256,128]{1,0:T(8,128)}) %reduce-scatter.3.cloned.1.call-update) | async-done | bytes 131088 | tf_op jit(solution)/shard_map/reduce_scatter | solution.py:95
  198.3 13.4 %all_gather.26 = bf16[256,512]{1,0:T(8,128)(2,1)} all-gather(bf16[256,128]{1,0:T(8,128)(2,1)S(1)} %add_convert_fusion.1), channel_id=1, replica_groups=mesh['walk'=2,'row'=4,'col'=4] {'col'}, dimensions={1}, use_global_device_ids=true | all-gather | bytes 327680 | tf_op jit(solution)/shard_map/all_gather | solution.py:97
  213.4 13.7 %all-gather.8.cloned.1.call-done = bf16[1024,512]{1,0:T(8,128)(2,1)} async-done(((bf16[256,512]{1,0:T(8,128)(2,1)}), bf16[1024,512]{1,0:T(8,128)(2,1)}) %all-gather.8.cloned.1.call-update) | async-done | bytes 1048592 | tf_op jit(solution)/shard_map/all_gather | solution.py:82
  228.6 132.6 %while.25 = (s32[]{:T(128)}, f32[8,32,512]{2,1,0:T(8,128)S(1)}, s32[8]{0:T(128)S(1)}, f32[256,512]{1,0:T(8,128)S(1)}, f32[256,512]{1,0:T(8,128)S(1)}, /*index=5*...) while((s32[]{:T(128)}, f32[8,32,512]{2,1,0:T(8,128)S(1)}, ...), condition=%wide.region_6.7_spmd, body=%wide.region_4.6_spmd.sunk | while | flops 4341088256 | bytes 55620052 | solution.py:39
  234.3 5.8 %multiply_convert_fusion.5 = bf16[8192,512]{1,0:T(8,128)(2,1)S(1)} fusion(f32[32,256,512]{2,1,0:T(8,128)S(1)} %add_add_fusion.5, f32[512]{0:T(512)S(1)} %copy-done.8, f32[8192]{0:T(1024)S(1)} %bitcast.107), kind=kLoop, calls=%fused_computation.12.clone.1 | loop fusion | flops 29360128 | bytes 25200640 | tf_op jit(solution)/shard_map/while/body/eval_jaxpr/convert_element_type | solution.py:31
  240.2 5.0 %bitcast_reduce_fusion.5 = f32[32,512]{1,0:T(8,128)S(1)} fusion(bf16[8192,512]{1,0:T(8,128)(2,1)S(1)} %multiply_convert_fusion.5, bf16[512,512]{1,0:T(8,128)(2,1)S(1)} %copy-done.3, f32[512]{0:T(512)S(1)} %bitcast.110), kind=kOutput, calls=%fused_computation.9.clone.1 | convolution fusion | flops 4303339520 | bytes 8980480 | tf_op jit(solution)/shard_map/while/body/eval_jaxpr/dot_general | solution.py:34
  250.9 5.8 %multiply_convert_fusion.5 = bf16[8192,512]{1,0:T(8,128)(2,1)S(1)} fusion(f32[32,256,512]{2,1,0:T(8,128)S(1)} %add_add_fusion.5, f32[512]{0:T(512)S(1)} %copy-done.8, f32[8192]{0:T(1024)S(1)} %bitcast.107), kind=kLoop, calls=%fused_computation.12.clone.1 | loop fusion | flops 29360128 | bytes 25200640 | tf_op jit(solution)/shard_map/while/body/eval_jaxpr/convert_element_type | solution.py:31
  256.7 5.0 %bitcast_reduce_fusion.5 = f32[32,512]{1,0:T(8,128)S(1)} fusion(bf16[8192,512]{1,0:T(8,128)(2,1)S(1)} %multiply_convert_fusion.5, bf16[512,512]{1,0:T(8,128)(2,1)S(1)} %copy-done.3, f32[512]{0:T(512)S(1)} %bitcast.110), kind=kOutput, calls=%fused_computation.9.clone.1 | convolution fusion | flops 4303339520 | bytes 8980480 | tf_op jit(solution)/shard_map/while/body/eval_jaxpr/dot_general | solution.py:34
  267.5 5.8 %multiply_convert_fusion.5 = bf16[8192,512]{1,0:T(8,128)(2,1)S(1)} fusion(f32[32,256,512]{2,1,0:T(8,128)S(1)} %add_add_fusion.5, f32[512]{0:T(512)S(1)} %copy-done.8, f32[8192]{0:T(1024)S(1)} %bitcast.107), kind=kLoop, calls=%fused_computation.12.clone.1 | loop fusion | flops 29360128 | bytes 25200640 | tf_op jit(solution)/shard_map/while/body/eval_jaxpr/convert_element_type | solution.py:31
  273.3 5.0 %bitcast_reduce_fusion.5 = f32[32,512]{1,0:T(8,128)S(1)} fusion(bf16[8192,512]{1,0:T(8,128)(2,1)S(1)} %multiply_convert_fusion.5, bf16[512,512]{1,0:T(8,128)(2,1)S(1)} %copy-done.3, f32[512]{0:T(512)S(1)} %bitcast.110), kind=kOutput, calls=%fused_computation.9.clone.1 | convolution fusion | flops 4303339520 | bytes 8980480 | tf_op jit(solution)/shard_map/while/body/eval_jaxpr/dot_general | solution.py:34
  284.1 5.8 %multiply_convert_fusion.5 = bf16[8192,512]{1,0:T(8,128)(2,1)S(1)} fusion(f32[32,256,512]{2,1,0:T(8,128)S(1)} %add_add_fusion.5, f32[512]{0:T(512)S(1)} %copy-done.8, f32[8192]{0:T(1024)S(1)} %bitcast.107), kind=kLoop, calls=%fused_computation.12.clone.1 | loop fusion | flops 29360128 | bytes 25200640 | tf_op jit(solution)/shard_map/while/body/eval_jaxpr/convert_element_type | solution.py:31
  289.9 5.0 %bitcast_reduce_fusion.5 = f32[32,512]{1,0:T(8,128)S(1)} fusion(bf16[8192,512]{1,0:T(8,128)(2,1)S(1)} %multiply_convert_fusion.5, bf16[512,512]{1,0:T(8,128)(2,1)S(1)} %copy-done.3, f32[512]{0:T(512)S(1)} %bitcast.110), kind=kOutput, calls=%fused_computation.9.clone.1 | convolution fusion | flops 4303339520 | bytes 8980480 | tf_op jit(solution)/shard_map/while/body/eval_jaxpr/dot_general | solution.py:34
  300.6 5.8 %multiply_convert_fusion.5 = bf16[8192,512]{1,0:T(8,128)(2,1)S(1)} fusion(f32[32,256,512]{2,1,0:T(8,128)S(1)} %add_add_fusion.5, f32[512]{0:T(512)S(1)} %copy-done.8, f32[8192]{0:T(1024)S(1)} %bitcast.107), kind=kLoop, calls=%fused_computation.12.clone.1 | loop fusion | flops 29360128 | bytes 25200640 | tf_op jit(solution)/shard_map/while/body/eval_jaxpr/convert_element_type | solution.py:31
  306.5 5.0 %bitcast_reduce_fusion.5 = f32[32,512]{1,0:T(8,128)S(1)} fusion(bf16[8192,512]{1,0:T(8,128)(2,1)S(1)} %multiply_convert_fusion.5, bf16[512,512]{1,0:T(8,128)(2,1)S(1)} %copy-done.3, f32[512]{0:T(512)S(1)} %bitcast.110), kind=kOutput, calls=%fused_computation.9.clone.1 | convolution fusion | flops 4303339520 | bytes 8980480 | tf_op jit(solution)/shard_map/while/body/eval_jaxpr/dot_general | solution.py:34
  317.2 5.8 %multiply_convert_fusion.5 = bf16[8192,512]{1,0:T(8,128)(2,1)S(1)} fusion(f32[32,256,512]{2,1,0:T(8,128)S(1)} %add_add_fusion.5, f32[512]{0:T(512)S(1)} %copy-done.8, f32[8192]{0:T(1024)S(1)} %bitcast.107), kind=kLoop, calls=%fused_computation.12.clone.1 | loop fusion | flops 29360128 | bytes 25200640 | tf_op jit(solution)/shard_map/while/body/eval_jaxpr/convert_element_type | solution.py:31
  323.1 5.0 %bitcast_reduce_fusion.5 = f32[32,512]{1,0:T(8,128)S(1)} fusion(bf16[8192,512]{1,0:T(8,128)(2,1)S(1)} %multiply_convert_fusion.5, bf16[512,512]{1,0:T(8,128)(2,1)S(1)} %copy-done.3, f32[512]{0:T(512)S(1)} %bitcast.110), kind=kOutput, calls=%fused_computation.9.clone.1 | convolution fusion | flops 4303339520 | bytes 8980480 | tf_op jit(solution)/shard_map/while/body/eval_jaxpr/dot_general | solution.py:34
  333.8 5.8 %multiply_convert_fusion.5 = bf16[8192,512]{1,0:T(8,128)(2,1)S(1)} fusion(f32[32,256,512]{2,1,0:T(8,128)S(1)} %add_add_fusion.5, f32[512]{0:T(512)S(1)} %copy-done.8, f32[8192]{0:T(1024)S(1)} %bitcast.107), kind=kLoop, calls=%fused_computation.12.clone.1 | loop fusion | flops 29360128 | bytes 25200640 | tf_op jit(solution)/shard_map/while/body/eval_jaxpr/convert_element_type | solution.py:31
  339.6 5.0 %bitcast_reduce_fusion.5 = f32[32,512]{1,0:T(8,128)S(1)} fusion(bf16[8192,512]{1,0:T(8,128)(2,1)S(1)} %multiply_convert_fusion.5, bf16[512,512]{1,0:T(8,128)(2,1)S(1)} %copy-done.3, f32[512]{0:T(512)S(1)} %bitcast.110), kind=kOutput, calls=%fused_computation.9.clone.1 | convolution fusion | flops 4303339520 | bytes 8980480 | tf_op jit(solution)/shard_map/while/body/eval_jaxpr/dot_general | solution.py:34
  350.4 5.8 %multiply_convert_fusion.5 = bf16[8192,512]{1,0:T(8,128)(2,1)S(1)} fusion(f32[32,256,512]{2,1,0:T(8,128)S(1)} %add_add_fusion.5, f32[512]{0:T(512)S(1)} %copy-done.8, f32[8192]{0:T(1024)S(1)} %bitcast.107), kind=kLoop, calls=%fused_computation.12.clone.1 | loop fusion | flops 29360128 | bytes 25200640 | tf_op jit(solution)/shard_map/while/body/eval_jaxpr/convert_element_type | solution.py:31
  356.2 5.0 %bitcast_reduce_fusion.5 = f32[32,512]{1,0:T(8,128)S(1)} fusion(bf16[8192,512]{1,0:T(8,128)(2,1)S(1)} %multiply_convert_fusion.5, bf16[512,512]{1,0:T(8,128)(2,1)S(1)} %copy-done.3, f32[512]{0:T(512)S(1)} %bitcast.110), kind=kOutput, calls=%fused_computation.9.clone.1 | convolution fusion | flops 4303339520 | bytes 8980480 | tf_op jit(solution)/shard_map/while/body/eval_jaxpr/dot_general | solution.py:34
  363.8 20.3 %reduce-scatter.5.cloned.1.call-done = f32[256,128]{1,0:T(8,128)} async-done(((f32[256,512]{1,0:T(8,128)}), f32[256,128]{1,0:T(8,128)}) %reduce-scatter.5.cloned.1.call-update) | async-done | bytes 131088 | tf_op jit(solution)/shard_map/reduce_scatter | solution.py:95
  385.0 12.8 %all_gather.28 = bf16[256,512]{1,0:T(8,128)(2,1)S(1)} all-gather(bf16[256,128]{1,0:T(8,128)(2,1)S(1)} %add_convert_fusion), channel_id=1, replica_groups=mesh['walk'=2,'row'=4,'col'=4] {'col'}, dimensions={1}, use_global_device_ids=true | all-gather | bytes 327680 | tf_op jit(solution)/shard_map/all_gather | solution.py:97
  398.2 9.3 %collective-permute-done = f32[256,256]{0,1:T(8,128)S(1)} collective-permute-done((f32[256,256]{0,1:T(8,128)S(1)}, f32[256,256]{0,1:T(8,128)S(1)}, u32[]{:S(2)}, u32[]{:S(2)}) %collective-permute-start) | collective-permute-done | bytes 262176 | tf_op jit(solution)/shard_map/ppermute | solution.py:101
  407.5 10.4 %collective-permute-done.1 = f32[256,256]{0,1:T(8,128)S(1)} collective-permute-done((f32[256,256]{0,1:T(8,128)S(1)}, f32[256,256]{0,1:T(8,128)S(1)}, u32[]{:S(2)}, u32[]{:S(2)}) %collective-permute-start.1) | collective-permute-done | bytes 262176 | tf_op jit(solution)/shard_map/ppermute | solution.py:101
  417.9 13.9 %collective-permute-done.2 = f32[256,256]{0,1:T(8,128)S(1)} collective-permute-done((f32[256,256]{0,1:T(8,128)S(1)}, f32[256,256]{0,1:T(8,128)S(1)}, u32[]{:S(2)}, u32[]{:S(2)}) %collective-permute-start.2) | collective-permute-done | bytes 262176 | tf_op jit(solution)/shard_map/ppermute | solution.py:101
  432.0 3.8 convolution_subtract_fusion
  435.8 3.9 all-gather.14.cloned.1.call-done
  439.7 18.2 %all-gather.12.cloned.1.call-done = f32[1024,256]{1,0:T(8,128)} async-done(((f32[256,256]{1,0:T(8,128)}), f32[1024,256]{1,0:T(8,128)}) %all-gather.12.cloned.1.call-update) | async-done | bytes 1048592 | tf_op jit(solution)/shard_map/all_gather | solution.py:120
  458.0 3.4 convolution_bitcast_fusion
  (233 shorter events, 100.6 us)
Async XLA Ops:
  7.2 390.7 %copy-start = (bf16[512,256]{1,0:T(8,128)(2,1)S(1)}, bf16[512,256]{1,0:T(8,128)(2,1)}, u32[]{:S(2)}) copy-start(bf16[512,256]{1,0:T(8,128)(2,1)} %param.25) | copy-start | bytes 786436
  7.2 32.2 %all-gather.6.cloned.1.call-start = ((), (), s32[]{:S(2)}) async-start(), calls=%async_computation.2 | async-start | bytes 1310720 | tf_op jit(solution)/shard_map/all_gather | solution.py:82
  23.9 173.5 %reduce-scatter.3.cloned.1.call-start = ((), (), s32[]{:S(2)}) async-start(), calls=%async_computation.3 | async-start | bytes 655360 | tf_op jit(solution)/shard_map/reduce_scatter | solution.py:95
  42.5 154.9 %copy-start.5 = (bf16[256,128]{1,0:T(8,128)(2,1)S(1)}, bf16[256,128]{1,0:T(8,128)(2,1)}, u32[]{:S(2)}) copy-start(bf16[256,128]{1,0:T(8,128)(2,1)} %param.16) | copy-start | bytes 196612
  42.5 5.6 %copy-start.7 = (f32[512]{0:T(512)S(1)}, f32[512]{0:T(512)}, u32[]{:S(2)}) copy-start(f32[512]{0:T(512)} %get-tuple-element.471) | copy-start | bytes 6148 | tf_op jit(solution)/shard_map/while
  47.3 6.7 %copy-start.4 = (bf16[512,512]{1,0:T(8,128)(2,1)S(1)}, bf16[512,512]{1,0:T(8,128)(2,1)}, u32[]{:S(2)}) copy-start(bf16[512,512]{1,0:T(8,128)(2,1)} %get-tuple-element.472) | copy-start | bytes 1572868 | tf_op jit(solution)/shard_map/while
  59.0 5.6 %copy-start.7 = (f32[512]{0:T(512)S(1)}, f32[512]{0:T(512)}, u32[]{:S(2)}) copy-start(f32[512]{0:T(512)} %get-tuple-element.471) | copy-start | bytes 6148 | tf_op jit(solution)/shard_map/while
  63.8 6.7 %copy-start.4 = (bf16[512,512]{1,0:T(8,128)(2,1)S(1)}, bf16[512,512]{1,0:T(8,128)(2,1)}, u32[]{:S(2)}) copy-start(bf16[512,512]{1,0:T(8,128)(2,1)} %get-tuple-element.472) | copy-start | bytes 1572868 | tf_op jit(solution)/shard_map/while
  75.6 5.6 %copy-start.7 = (f32[512]{0:T(512)S(1)}, f32[512]{0:T(512)}, u32[]{:S(2)}) copy-start(f32[512]{0:T(512)} %get-tuple-element.471) | copy-start | bytes 6148 | tf_op jit(solution)/shard_map/while
  80.3 6.7 %copy-start.4 = (bf16[512,512]{1,0:T(8,128)(2,1)S(1)}, bf16[512,512]{1,0:T(8,128)(2,1)}, u32[]{:S(2)}) copy-start(bf16[512,512]{1,0:T(8,128)(2,1)} %get-tuple-element.472) | copy-start | bytes 1572868 | tf_op jit(solution)/shard_map/while
  92.1 5.6 %copy-start.7 = (f32[512]{0:T(512)S(1)}, f32[512]{0:T(512)}, u32[]{:S(2)}) copy-start(f32[512]{0:T(512)} %get-tuple-element.471) | copy-start | bytes 6148 | tf_op jit(solution)/shard_map/while
  96.8 6.7 %copy-start.4 = (bf16[512,512]{1,0:T(8,128)(2,1)S(1)}, bf16[512,512]{1,0:T(8,128)(2,1)}, u32[]{:S(2)}) copy-start(bf16[512,512]{1,0:T(8,128)(2,1)} %get-tuple-element.472) | copy-start | bytes 1572868 | tf_op jit(solution)/shard_map/while
  108.6 5.6 %copy-start.7 = (f32[512]{0:T(512)S(1)}, f32[512]{0:T(512)}, u32[]{:S(2)}) copy-start(f32[512]{0:T(512)} %get-tuple-element.471) | copy-start | bytes 6148 | tf_op jit(solution)/shard_map/while
  113.3 6.7 %copy-start.4 = (bf16[512,512]{1,0:T(8,128)(2,1)S(1)}, bf16[512,512]{1,0:T(8,128)(2,1)}, u32[]{:S(2)}) copy-start(bf16[512,512]{1,0:T(8,128)(2,1)} %get-tuple-element.472) | copy-start | bytes 1572868 | tf_op jit(solution)/shard_map/while
  125.1 5.6 %copy-start.7 = (f32[512]{0:T(512)S(1)}, f32[512]{0:T(512)}, u32[]{:S(2)}) copy-start(f32[512]{0:T(512)} %get-tuple-element.471) | copy-start | bytes 6148 | tf_op jit(solution)/shard_map/while
  129.8 6.7 %copy-start.4 = (bf16[512,512]{1,0:T(8,128)(2,1)S(1)}, bf16[512,512]{1,0:T(8,128)(2,1)}, u32[]{:S(2)}) copy-start(bf16[512,512]{1,0:T(8,128)(2,1)} %get-tuple-element.472) | copy-start | bytes 1572868 | tf_op jit(solution)/shard_map/while
  141.6 5.6 %copy-start.7 = (f32[512]{0:T(512)S(1)}, f32[512]{0:T(512)}, u32[]{:S(2)}) copy-start(f32[512]{0:T(512)} %get-tuple-element.471) | copy-start | bytes 6148 | tf_op jit(solution)/shard_map/while
  146.3 6.7 %copy-start.4 = (bf16[512,512]{1,0:T(8,128)(2,1)S(1)}, bf16[512,512]{1,0:T(8,128)(2,1)}, u32[]{:S(2)}) copy-start(bf16[512,512]{1,0:T(8,128)(2,1)} %get-tuple-element.472) | copy-start | bytes 1572868 | tf_op jit(solution)/shard_map/while
  158.1 5.6 %copy-start.7 = (f32[512]{0:T(512)S(1)}, f32[512]{0:T(512)}, u32[]{:S(2)}) copy-start(f32[512]{0:T(512)} %get-tuple-element.471) | copy-start | bytes 6148 | tf_op jit(solution)/shard_map/while
  162.8 6.7 %copy-start.4 = (bf16[512,512]{1,0:T(8,128)(2,1)S(1)}, bf16[512,512]{1,0:T(8,128)(2,1)}, u32[]{:S(2)}) copy-start(bf16[512,512]{1,0:T(8,128)(2,1)} %get-tuple-element.472) | copy-start | bytes 1572868 | tf_op jit(solution)/shard_map/while
  174.6 0.8 copy-start.2
  175.4 51.7 %all-gather.8.cloned.1.call-start = ((), (), s32[]{:S(2)}) async-start(), calls=%async_computation.4 | async-start | bytes 1310720 | tf_op jit(solution)/shard_map/all_gather | solution.py:82
  211.8 172.3 %reduce-scatter.5.cloned.1.call-start = ((), (), s32[]{:S(2)}) async-start(), calls=%async_computation.5 | async-start | bytes 655360 | tf_op jit(solution)/shard_map/reduce_scatter | solution.py:95
  228.6 5.7 %copy-start.8 = (f32[512]{0:T(512)S(1)}, f32[512]{0:T(512)}, u32[]{:S(2)}) copy-start(f32[512]{0:T(512)} %get-tuple-element.525) | copy-start | bytes 6148 | tf_op jit(solution)/shard_map/while
  233.4 6.7 %copy-start.3 = (bf16[512,512]{1,0:T(8,128)(2,1)S(1)}, bf16[512,512]{1,0:T(8,128)(2,1)}, u32[]{:S(2)}) copy-start(bf16[512,512]{1,0:T(8,128)(2,1)} %get-tuple-element.526) | copy-start | bytes 1572868 | tf_op jit(solution)/shard_map/while
  245.2 5.7 %copy-start.8 = (f32[512]{0:T(512)S(1)}, f32[512]{0:T(512)}, u32[]{:S(2)}) copy-start(f32[512]{0:T(512)} %get-tuple-element.525) | copy-start | bytes 6148 | tf_op jit(solution)/shard_map/while
  250.0 6.7 %copy-start.3 = (bf16[512,512]{1,0:T(8,128)(2,1)S(1)}, bf16[512,512]{1,0:T(8,128)(2,1)}, u32[]{:S(2)}) copy-start(bf16[512,512]{1,0:T(8,128)(2,1)} %get-tuple-element.526) | copy-start | bytes 1572868 | tf_op jit(solution)/shard_map/while
  261.8 5.7 %copy-start.8 = (f32[512]{0:T(512)S(1)}, f32[512]{0:T(512)}, u32[]{:S(2)}) copy-start(f32[512]{0:T(512)} %get-tuple-element.525) | copy-start | bytes 6148 | tf_op jit(solution)/shard_map/while
  266.6 6.7 %copy-start.3 = (bf16[512,512]{1,0:T(8,128)(2,1)S(1)}, bf16[512,512]{1,0:T(8,128)(2,1)}, u32[]{:S(2)}) copy-start(bf16[512,512]{1,0:T(8,128)(2,1)} %get-tuple-element.526) | copy-start | bytes 1572868 | tf_op jit(solution)/shard_map/while
  278.4 5.7 %copy-start.8 = (f32[512]{0:T(512)S(1)}, f32[512]{0:T(512)}, u32[]{:S(2)}) copy-start(f32[512]{0:T(512)} %get-tuple-element.525) | copy-start | bytes 6148 | tf_op jit(solution)/shard_map/while
  283.2 6.7 %copy-start.3 = (bf16[512,512]{1,0:T(8,128)(2,1)S(1)}, bf16[512,512]{1,0:T(8,128)(2,1)}, u32[]{:S(2)}) copy-start(bf16[512,512]{1,0:T(8,128)(2,1)} %get-tuple-element.526) | copy-start | bytes 1572868 | tf_op jit(solution)/shard_map/while
  295.0 5.7 %copy-start.8 = (f32[512]{0:T(512)S(1)}, f32[512]{0:T(512)}, u32[]{:S(2)}) copy-start(f32[512]{0:T(512)} %get-tuple-element.525) | copy-start | bytes 6148 | tf_op jit(solution)/shard_map/while
  299.8 6.7 %copy-start.3 = (bf16[512,512]{1,0:T(8,128)(2,1)S(1)}, bf16[512,512]{1,0:T(8,128)(2,1)}, u32[]{:S(2)}) copy-start(bf16[512,512]{1,0:T(8,128)(2,1)} %get-tuple-element.526) | copy-start | bytes 1572868 | tf_op jit(solution)/shard_map/while
  311.5 5.7 %copy-start.8 = (f32[512]{0:T(512)S(1)}, f32[512]{0:T(512)}, u32[]{:S(2)}) copy-start(f32[512]{0:T(512)} %get-tuple-element.525) | copy-start | bytes 6148 | tf_op jit(solution)/shard_map/while
  316.4 6.7 %copy-start.3 = (bf16[512,512]{1,0:T(8,128)(2,1)S(1)}, bf16[512,512]{1,0:T(8,128)(2,1)}, u32[]{:S(2)}) copy-start(bf16[512,512]{1,0:T(8,128)(2,1)} %get-tuple-element.526) | copy-start | bytes 1572868 | tf_op jit(solution)/shard_map/while
  328.1 5.7 %copy-start.8 = (f32[512]{0:T(512)S(1)}, f32[512]{0:T(512)}, u32[]{:S(2)}) copy-start(f32[512]{0:T(512)} %get-tuple-element.525) | copy-start | bytes 6148 | tf_op jit(solution)/shard_map/while
  332.9 6.7 %copy-start.3 = (bf16[512,512]{1,0:T(8,128)(2,1)S(1)}, bf16[512,512]{1,0:T(8,128)(2,1)}, u32[]{:S(2)}) copy-start(bf16[512,512]{1,0:T(8,128)(2,1)} %get-tuple-element.526) | copy-start | bytes 1572868 | tf_op jit(solution)/shard_map/while
  344.7 5.7 %copy-start.8 = (f32[512]{0:T(512)S(1)}, f32[512]{0:T(512)}, u32[]{:S(2)}) copy-start(f32[512]{0:T(512)} %get-tuple-element.525) | copy-start | bytes 6148 | tf_op jit(solution)/shard_map/while
  349.5 6.7 %copy-start.3 = (bf16[512,512]{1,0:T(8,128)(2,1)S(1)}, bf16[512,512]{1,0:T(8,128)(2,1)}, u32[]{:S(2)}) copy-start(bf16[512,512]{1,0:T(8,128)(2,1)} %get-tuple-element.526) | copy-start | bytes 1572868 | tf_op jit(solution)/shard_map/while
  361.3 0.8 copy-start.1
  362.1 69.9 %all-gather.10.cloned.1.call-start = ((), (), s32[]{:S(2)}) async-start(), calls=%async_computation.6 | async-start | bytes 1310720 | tf_op jit(solution)/shard_map/all_gather | solution.py:108
  362.7 77.0 %all-gather.14.cloned.1.call-start = ((), (), s32[]{:S(2)}) async-start(), calls=%async_computation.8 | async-start | bytes 1310720 | tf_op jit(solution)/shard_map/all_gather | solution.py:116
  385.0 77.1 %copy-start.6 = (bf16[256,128]{1,0:T(8,128)(2,1)}, bf16[256,128]{1,0:T(8,128)(2,1)S(1)}, u32[]{:S(2)}) copy-start(bf16[256,128]{1,0:T(8,128)(2,1)S(1)} %add_convert_fusion) | copy-start | bytes 196612
  398.1 9.3 %collective-permute-start = (f32[256,256]{0,1:T(8,128)S(1)}, f32[256,256]{0,1:T(8,128)S(1)}, u32[]{:S(2)}, u32[]{:S(2)}) collective-permute-start(f32[256,256]{0,1:T(8,128)S(1)} %convolution_multiply_fusion), channel_id=1, source_target_pairs={{0,1},{1,2},{2,3},{3,0},{4,5},{5,6},{6,7},{7,4},{8,9},{9,10},{10,1... | collective-permute-start | bytes 786440 | tf_op jit(solution)/shard_map/ppermute | solution.py:101
  407.4 10.4 %collective-permute-start.1 = (f32[256,256]{0,1:T(8,128)S(1)}, f32[256,256]{0,1:T(8,128)S(1)}, u32[]{:S(2)}, u32[]{:S(2)}) collective-permute-start(f32[256,256]{0,1:T(8,128)S(1)} %collective-permute-done), channel_id=1, source_target_pairs={{0,1},{1,2},{2,3},{3,0},{4,5},{5,6},{6,7},{7,4},{8,9},{9,10},{10,1... | collective-permute-start | bytes 786440 | tf_op jit(solution)/shard_map/ppermute | solution.py:101
  407.5 50.5 %all-gather.12.cloned.1.call-start = ((), (), s32[]{:S(2)}) async-start(), calls=%async_computation.7 | async-start | bytes 1310720 | tf_op jit(solution)/shard_map/all_gather | solution.py:120
  417.9 13.9 %collective-permute-start.2 = (f32[256,256]{0,1:T(8,128)S(1)}, f32[256,256]{0,1:T(8,128)S(1)}, u32[]{:S(2)}, u32[]{:S(2)}) collective-permute-start(f32[256,256]{0,1:T(8,128)S(1)} %collective-permute-done.1), channel_id=1, source_target_pairs={{0,1},{1,2},{2,3},{3,0},{4,5},{5,6},{6,7},{7,4},{8,9},{9,10},{10,1... | collective-permute-start | bytes 786440 | tf_op jit(solution)/shard_map/ppermute | solution.py:101
Sparse Core Ops, SparseCore 0:
  24.0 15.3 all-gather.5
  175.5 21.8 reduce-scatter.2
  211.9 15.1 all-gather.7
  362.2 21.8 reduce-scatter.4
  385.5 14.9 all-gather.9
  407.6 32.0 all-gather.13
  441.8 16.0 all-gather.11
